TPU v7x, 128 devices: a whole 4x4x4 slice. The times are simulated.
128 devices in a mesh: sub: 16 (over x, y), row: 8 (over z, core).
Axes of the slice: x: 4, y: 4, z: 4, core: 2. Of those that a mesh axis runs over, the one named last changes fastest.
Arguments:
- sigma_top: float32 [6144, 6144], P('row', 'sub'), may hold values from -2 to 4, as said below
- coupling: float32 [16, 6144, 768], P('sub', 'row'), may hold values from -0.16 to 0.16
- child_inverse: float32 [16, 768, 768], P('sub', 'row'), may hold values from -1 to 10, as said below
- tile_mask: int32 [16, 24], P('sub'), may hold values 0 or 1
- obs_node: int32 [32768], P(('sub', 'row')), may hold values from 0 to 12287
- obs_noise: float32 [32768], P(('sub', 'row')), may hold values from 0.05 to 2
Outputs:
- sep_child: float32 [16, 6144, 768], P('sub', 'row')
- child_block: float32 [16, 768, 768], P('sub', 'row')
- loo_var: float32 [32768], P(('sub', 'row'))
Inputs may be any that keep to these rules, and one draw needn't show every extreme that they name: sigma_top is exactly symmetric. Each child_inverse[c] is exactly symmetric.
All inputs are finite; a program needn't handle non-finite values. No bound on the sum of `tile_mask` on one device may be relied on, other than what follows from the above.
Results may differ from a plain program's by a relative error of at most 0.000073.
Values sent between devices are 32-bit elements; how exact they have to be, the bound alone decides.
No kernel may reach another device: no remote copies, remote signals or barrier semaphores. Data moves between devices by JAX's collectives and lax.ppermute only.
A program may use at most 128 MiB of HBM per device.

v0:
```python
import jax
import jax.numpy as jnp
from jax import lax
from jax.sharding import PartitionSpec as P

TILE = 256


def local(sigma_top, coupling, child_inverse, tile_mask, obs_node, obs_noise):
    highest = lax.Precision.HIGHEST
    rows_here = coupling.shape[1]
    width_here = child_inverse.shape[1]
    tiles_here = rows_here // TILE
    row_index = lax.axis_index("row")
    mask_here = lax.dynamic_slice_in_dim(tile_mask[0], row_index * tiles_here, tiles_here)
    row_mask = jnp.repeat(mask_here, TILE).astype(jnp.float32)
    masked = coupling[0] * row_mask[:, None]
    gathered = lax.all_gather(masked, "row", axis=0, tiled=True)
    product = jnp.dot(
        lax.all_gather(sigma_top, "sub", axis=1, tiled=True),
        gathered,
        precision=highest,
        preferred_element_type=jnp.float32,
    )
    sep_part = -product
    update = lax.psum_scatter(
        lax.dot_general(
            masked,
            sep_part,
            (((0,), (0,)), ((), ())),
            precision=highest,
            preferred_element_type=jnp.float32,
        ),
        "row",
        scatter_dimension=0,
        tiled=True,
    )
    block_here = child_inverse[0] - update
    own_cols = lax.dynamic_slice_in_dim(block_here, row_index * width_here, width_here, 1)
    own_diag = jnp.diagonal(own_cols)
    every_var = lax.all_gather(own_diag, ("sub", "row"), axis=0, tiled=True)
    loo_var = every_var[obs_node] + obs_noise
    return (sep_part[None], block_here[None], loo_var)


def solution(mesh):
    placed = (
        P("row", "sub"),
        P("sub", "row", None),
        P("sub", "row", None),
        P("sub", None),
        P(("sub", "row")),
        P(("sub", "row")),
    )
    return jax.shard_map(
        local,
        mesh=mesh,
        in_specs=placed,
        out_specs=(P("sub", "row", None), P("sub", "row", None), P(("sub", "row"))),
        check_vma=False,
    )
```

profile of v0, /device:TPU:1, one launch (start us, length us, event | category | flops | bytes accessed | tf_op | source)
XLA Modules:
  0.0 450.1 jit_solution(1674996634150140336)
XLA Ops:
  7.2 0.0 all-gather.3.cloned.1.call-start
  7.2 0.7 convert_bitcast_fusion
  7.9 0.1 broadcast_in_dim.17
  8.0 3.3 bitcast_multiply_fusion
  11.3 0.0 all-gather.5.cloned.1.call-start
  11.4 0.7 all-gather.5.cloned.1.call-update
  12.1 0.0 reduce-scatter.2.cloned.1.call-start
  12.2 97.0 %all-gather.3.cloned.1.call-done = f32[6144,768]{1,0:T(8,128)} async-done(((f32[768,768]{1,0:T(8,128)}), f32[6144,768]{1,0:T(8,128)}) %all-gather.3.cloned.1.call-update) | async-done | bytes 18874384 | tf_op jit(solution)/shard_map/all_gather | solution.py:18
  109.1 124.2 %all-gather.5.cloned.1.call-done = f32[768,6144]{1,0:T(8,128)} async-done(((f32[768,384]{1,0:T(8,128)}), f32[768,6144]{1,0:T(8,128)}) %all-gather.5.cloned.1.call-update) | async-done | bytes 18874384 | tf_op jit(solution)/shard_map/all_gather | solution.py:20
  233.4 92.2 %fusion.2 = f32[768,768]{1,0:T(8,128)S(1)} fusion(f32[6144,768]{1,0:T(8,128)} %all-gather.3.cloned.1.call-done, f32[768,6144]{1,0:T(8,128)} %all-gather.5.cloned.1.call-done), kind=kOutput, calls=%fused_computation.12 | convolution fusion | flops 43486543872 | bytes 40108032 | tf_op jit(solution)/shard_map/dot_general | solution.py:19
  325.5 1.4 copy-done.1
  326.9 12.5 %fusion = f32[768,768]{1,0:T(8,128)} fusion(f32[768,768]{1,0:T(8,128)S(1)} %copy-done, f32[768,768]{1,0:T(8,128)S(1)} %fusion.2), kind=kOutput, calls=%fused_computation.3 | convolution fusion | flops 5436407808 | bytes 7077888 | tf_op jit(solution)/shard_map/dot_general | solution.py:27
  339.5 0.6 copy-done.6
  340.2 1.0 copy-done.2
  341.2 1.6 negate_bitcast_fusion
  342.7 3.1 copy.10
  345.8 24.8 %reduce-scatter.2.cloned.1.call-done = f32[96,768]{1,0:T(8,128)} async-done(((f32[768,768]{1,0:T(8,128)}), f32[96,768]{1,0:T(8,128)}) %reduce-scatter.2.cloned.1.call-update) | async-done | bytes 294928 | tf_op jit(solution)/shard_map/reduce_scatter | solution.py:26
  370.6 1.0 bitcast_subtract_fusion
  371.6 0.1 constant_dynamic-slice_fusion
  371.7 1.2 gather_fusion
  373.0 0.3 dynamic-update-slice
  373.2 68.1 %all-reduce = f32[12288]{0:T(1024)S(1)} all-reduce(f32[12288]{0:T(1024)S(1)} %dynamic-update-slice), channel_id=1, replica_groups=mesh['sub'=16,'row'=8] {'sub','row'}, use_global_device_ids=true, to_apply=%add | all-reduce | flops 12288 | bytes 98304
  441.3 1.7 gather_fusion.1
  443.1 0.6 add.25
  (18 shorter events, 0.1 us)
Async XLA Ops:
  7.2 102.0 %all-gather.3.cloned.1.call-start = ((), (), s32[]{:S(2)}) async-start(), calls=%async_computation.1 | async-start | bytes 21233664 | tf_op jit(solution)/shard_map/all_gather | solution.py:18
  11.3 222.0 %all-gather.5.cloned.1.call-start = ((), (), s32[]{:S(2)}) async-start(), calls=%async_computation.2 | async-start | bytes 20054016 | tf_op jit(solution)/shard_map/all_gather | solution.py:20
  12.1 314.8 %copy-start = (f32[768,768]{1,0:T(8,128)S(1)}, f32[768,768]{1,0:T(8,128)}, u32[]{:S(2)}) copy-start(f32[768,768]{1,0:T(8,128)} %bitcast_multiply_fusion) | copy-start | bytes 7077892
  12.1 358.5 %reduce-scatter.2.cloned.1.call-start = ((), (), s32[]{:S(2)}) async-start(), calls=%async_computation.3 | async-start | bytes 2654208 | tf_op jit(solution)/shard_map/reduce_scatter | solution.py:26
  325.5 1.4 copy-start.1
  339.5 0.7 copy-start.6
  339.5 1.7 copy-start.2
  342.7 27.9 %copy-start.4 = (f32[1,96,768]{2,1,0:T(8,128)S(1)}, f32[1,96,768]{2,1,0:T(8,128)}, u32[]{:S(2)}) copy-start(f32[1,96,768]{2,1,0:T(8,128)} %param.8) | copy-start | bytes 884740
  345.8 97.2 %copy-start.5 = (f32[256]{0:T(256)S(1)}, f32[256]{0:T(256)}, u32[]{:S(2)}) copy-start(f32[256]{0:T(256)} %param.11) | copy-start | bytes 3076
  371.6 72.0 %copy-start.3 = (f32[96,768]{1,0:T(8,128)}, f32[96,768]{1,0:T(8,128)S(1)}, u32[]{:S(2)}) copy-start(f32[96,768]{1,0:T(8,128)S(1)} %bitcast_subtract_fusion) | copy-start | bytes 884740
Sparse Core Ops, SparseCore 0:
  11.5 97.6 all-gather.2
  111.3 121.9 all-gather.4
  339.6 30.9 reduce-scatter.1
where the time goes:
time: 450 us
  waiting for transfers between devices  247 us (55%)
  matrix products  105 us (23%)
  blocking collectives  68.1 us (15%)
  between operations  13.8 us (3%)
  local copies, waits for them, and re-layouts  9.55 us (2%)
  other arithmetic  7.17 us (2%)
    all_gather x1, waiting for transfers between devices, local(): lax.all_gather(sigma_top, 'sub', axis=1, tiled=True)  124 us
    all_gather x1, waiting for transfers between devices, local(): gathered = lax.all_gather(masked, 'row', axis=0, tiled=True)  97 us
    dot_general x1, matrix products, local(): jnp.dot(lax.all_gather(sigma_top, 'sub', axis=1, tiled=True), gathered, p...  92.2 us
    unnamed x1, blocking collectives  68.1 us
    reduce_scatter x1, waiting for transfers between devices, local(): lax.psum_scatter(lax.dot_general(masked, sep_part, (((0,), (0,)), ((), ()...  24.8 us
    dot_general x1, matrix products, local(): lax.dot_general(masked, sep_part, (((0,), (0,)), ((), ())), precision=hig...  12.5 us
  transfers between devices with their start and end apart: 3, of which 3 were waited for; matrix products, arithmetic and copies ran while one was open for 1% of the time, Pallas kernels for 0%

commit v1 on v0

--- a/solution.py
+++ b/solution.py
@@ -17,7 +17,9 @@
     masked = coupling[0] * row_mask[:, None]
     gathered = lax.all_gather(masked, "row", axis=0, tiled=True)
     product = jnp.dot(
-        lax.all_gather(sigma_top, "sub", axis=1, tiled=True),
+        jnp.concatenate(
+            lax.all_to_all(jnp.stack([sigma_top] * lax.axis_size("sub")), "sub", 0, 0), axis=1
+        ),
         gathered,
         precision=highest,
         preferred_element_type=jnp.float32,

time: 450 us -> 414 us (0.920)
  waiting for transfers between devices: 247 us -> 27.3 us
  blocking collectives: 68.1 us -> 285 us
  matrix products: 105 us -> 63.6 us
  local copies, waits for them, and re-layouts: 9.55 us -> 16.9 us
    all_to_all x0 -> x1, blocking collectives: none -> 216 us  [local(): lax.all_to_all(jnp.stack([sigma_top] * lax.axis_size('sub')), 'sub', 0, 0)]
    all_gather x1 -> x0, waiting for transfers between devices: 124 us -> none  [local(): lax.all_gather(sigma_top, 'sub', axis=1, tiled=True)]
    all_gather x1, waiting for transfers between devices: 97 us -> 0.01 us  [local(): gathered = lax.all_gather(masked, 'row', axis=0, tiled=True)]
    dot_general x1, matrix products: 92.2 us -> 51 us  [local(): jnp.dot(jnp.concatenate(lax.all_to_all(jnp.stack([sigma_top] * lax.axis_s...]
    another operation x0 -> x1, local copies, waits for them, and re-layouts: none -> 8.16 us  [local(): jnp.stack([sigma_top] * lax.axis_size('sub'))]
  transfers between devices with their start and end apart: 3 -> 2, of which waited for: 3 -> 1; matrix products, arithmetic and copies ran while one was open for 1% -> 3% of each run, Pallas kernels for 0% -> 0%
where the time goes in v1:
time: 414 us
  blocking collectives  285 us (69%)
  matrix products  63.6 us (15%)
  waiting for transfers between devices  27.3 us (7%)
  local copies, waits for them, and re-layouts  16.9 us (4%)
  between operations  14.1 us (3%)
  other arithmetic  7.16 us (2%)
    all_to_all x1, blocking collectives, local(): lax.all_to_all(jnp.stack([sigma_top] * lax.axis_size('sub')), 'sub', 0, 0)  216 us
    unnamed x1, blocking collectives  68.1 us
    dot_general x1, matrix products, local(): jnp.dot(jnp.concatenate(lax.all_to_all(jnp.stack([sigma_top] * lax.axis_s...  51 us
    reduce_scatter x1, waiting for transfers between devices, local(): lax.psum_scatter(lax.dot_general(masked, sep_part, (((0,), (0,)), ((), ()...  27.3 us
    dot_general x1, matrix products, local(): lax.dot_general(masked, sep_part, (((0,), (0,)), ((), ())), precision=hig...  12.5 us
  transfers between devices with their start and end apart: 2, of which 1 were waited for; matrix products, arithmetic and copies ran while one was open for 3% of the time, Pallas kernels for 0%

profile of v1, /device:TPU:1, one launch (start us, length us, event | category | flops | bytes accessed | tf_op | source)
XLA Modules:
  0.0 413.7 jit_solution(2380655108738818690)
XLA Ops:
  7.2 0.0 all-gather.2.cloned.1.call-start
  7.2 0.7 convert_bitcast_fusion
  7.9 0.1 broadcast_in_dim.17
  8.0 3.3 bitcast_multiply_fusion
  11.3 0.0 all-gather.2.cloned.1.call-update
  11.3 0.0 reduce-scatter.2.cloned.1.call-start
  11.4 1.2 copy-done.1
  12.6 0.4 copy.10
  13.0 8.2 %stack.2 = f32[16,768,384]{1,2,0:T(8,128)} broadcast(f32[768,384]{0,1:T(8,128)S(1)} %copy.10), dimensions={1,2} | broadcast | bytes 20054016 | tf_op jit(solution)/shard_map/stack | solution.py:21
  21.1 216.5 %all_to_all.5 = f32[16,768,384]{1,2,0:T(8,128)} all-to-all(f32[16,768,384]{1,2,0:T(8,128)} %stack.2), channel_id=1, replica_groups=mesh['sub'=16,'row'=8] {'sub'}, dimensions={0} | all-to-all | bytes 37748736 | tf_op jit(solution)/shard_map/all_to_all | solution.py:21
  237.6 51.0 %fusion.2 = f32[768,768]{1,0:T(8,128)S(1)} fusion(f32[6144,768]{1,0:T(8,128)} %all-gather.2.cloned.1.call-done, f32[768,6144]{0,1:T(8,128)} %bitcast.19), kind=kOutput, calls=%fused_computation.12 | convolution fusion | flops 43486543872 | bytes 40108032 | tf_op jit(solution)/shard_map/dot_general | solution.py:19
  288.7 12.5 %fusion = f32[768,768]{1,0:T(8,128)} fusion(f32[768,768]{1,0:T(8,128)S(1)} %copy-done, f32[768,768]{1,0:T(8,128)S(1)} %fusion.2), kind=kOutput, calls=%fused_computation.3 | convolution fusion | flops 5436407808 | bytes 7077888 | tf_op jit(solution)/shard_map/dot_general | solution.py:29
  301.2 0.0 reduce-scatter.2.cloned.1.call-update
  301.2 0.6 copy-done.5
  301.9 1.6 negate_bitcast_fusion
  303.5 3.1 copy.11
  306.5 27.3 %reduce-scatter.2.cloned.1.call-done = f32[96,768]{1,0:T(8,128)} async-done(((f32[768,768]{1,0:T(8,128)}), f32[96,768]{1,0:T(8,128)}) %reduce-scatter.2.cloned.1.call-update) | async-done | bytes 294928 | tf_op jit(solution)/shard_map/reduce_scatter | solution.py:28
  333.8 1.0 bitcast_subtract_fusion
  334.8 0.1 constant_dynamic-slice_fusion
  334.9 1.2 gather_fusion
  336.2 0.3 dynamic-update-slice
  336.5 68.1 %all-reduce = f32[12288]{0:T(1024)S(1)} all-reduce(f32[12288]{0:T(1024)S(1)} %dynamic-update-slice), channel_id=1, replica_groups=mesh['sub'=16,'row'=8] {'sub','row'}, use_global_device_ids=true, to_apply=%add | all-reduce | flops 12288 | bytes 98304
  404.5 1.7 gather_fusion.1
  406.3 0.6 add.25
  (16 shorter events, 0.1 us)
Async XLA Ops:
  7.2 230.4 %all-gather.2.cloned.1.call-start = ((), (), s32[]{:S(2)}) async-start(), calls=%async_computation.2 | async-start | bytes 21233664 | tf_op jit(solution)/shard_map/all_gather | solution.py:18
  11.3 1.3 copy-start.1
  11.3 322.5 %reduce-scatter.2.cloned.1.call-start = ((), (), s32[]{:S(2)}) async-start(), calls=%async_computation.3 | async-start | bytes 2654208 | tf_op jit(solution)/shard_map/reduce_scatter | solution.py:28
  237.6 51.1 %copy-start = (f32[768,768]{1,0:T(8,128)S(1)}, f32[768,768]{1,0:T(8,128)}, u32[]{:S(2)}) copy-start(f32[768,768]{1,0:T(8,128)} %bitcast_multiply_fusion) | copy-start | bytes 7077892
  301.2 0.7 copy-start.5
  303.5 30.4 %copy-start.3 = (f32[1,96,768]{2,1,0:T(8,128)S(1)}, f32[1,96,768]{2,1,0:T(8,128)}, u32[]{:S(2)}) copy-start(f32[1,96,768]{2,1,0:T(8,128)} %param.8) | copy-start | bytes 884740
  306.5 99.7 %copy-start.4 = (f32[256]{0:T(256)S(1)}, f32[256]{0:T(256)}, u32[]{:S(2)}) copy-start(f32[256]{0:T(256)} %param.11) | copy-start | bytes 3076
  334.8 72.0 %copy-start.2 = (f32[96,768]{1,0:T(8,128)}, f32[96,768]{1,0:T(8,128)S(1)}, u32[]{:S(2)}) copy-start(f32[96,768]{1,0:T(8,128)S(1)} %bitcast_subtract_fusion) | copy-start | bytes 884740
Sparse Core Ops, SparseCore 0:
  11.5 97.6 all-gather.1
  301.3 32.4 reduce-scatter.1
